TPU v7x, 32 devices: a whole 2x2x4 slice. The times are simulated.
32 devices in a mesh: parts: 1, row: 16 (over z, y, x), chan: 1, sub: 2 (over core).
Axes of the slice: x: 2, y: 2, z: 4, core: 2. Of those that a mesh axis runs over, the one named last changes fastest.
Arguments:
- pair: bfloat16 [448, 448, 128], P(('parts', 'row', 'sub'), 'chan'), may hold values from -6 to 6
- pair_mask: int32 [448, 448], P(('parts', 'row', 'sub'), 'chan'), may hold values 0 or 1
- out_in_gain: float32 [128], replicated, may hold values from 0.5 to 1.5
- out_proj: bfloat16 [128, 640], replicated, may hold values from -0.5 to 0.5
- out_mid_gain: float32 [128], replicated, may hold values from 0.5 to 1.5
- out_final: bfloat16 [128, 128], replicated, may hold values from -0.5 to 0.5
- in_in_gain: float32 [128], replicated, may hold values from 0.5 to 1.5
- in_proj: bfloat16 [128, 640], replicated, may hold values from -0.5 to 0.5
- in_mid_gain: float32 [128], replicated, may hold values from 0.5 to 1.5
- in_final: bfloat16 [128, 128], replicated, may hold values from -0.5 to 0.5
Outputs:
- updated: bfloat16 [448, 448, 128], P(('parts', 'row', 'sub'), 'chan')
All inputs are finite; a program needn't handle non-finite values. No bound on the sum of `pair_mask` on one device may be relied on, other than what follows from the above.
Results may differ from a plain program's by a relative error of at most 0.014.
Values may be sent and summed in bfloat16 or wider, within the bound.
A program may use at most 192 MiB of HBM per device.

v0:
```python
import jax
import jax.numpy as jnp
from jax import lax
from jax.sharding import PartitionSpec as P


def norm_last(values, gain):
    mean = jnp.mean(values, axis=-1, keepdims=True)
    var = jnp.mean((values - mean) ** 2, axis=-1, keepdims=True)
    return (values - mean) / jnp.sqrt(var + 1e-05) * gain


def project(pair, pair_mask, in_gain, proj, left_form, right_form, left_across):
    hidden = (proj.shape[1] - pair.shape[2]) // 4
    normed = norm_last(pair.astype(jnp.float32), in_gain).astype(jnp.bfloat16)
    keep = pair_mask.astype(jnp.float32)
    left_raw = jnp.einsum(
        left_form, normed, proj[:, : 2 * hidden], preferred_element_type=jnp.float32
    )
    right_raw = jnp.einsum(
        right_form, normed, proj[:, 2 * hidden : 4 * hidden], preferred_element_type=jnp.float32
    )
    left_keep = keep.T[None] if left_across else keep[None]
    left = (jax.nn.sigmoid(left_raw[:hidden]) * left_raw[hidden:] * left_keep).astype(jnp.bfloat16)
    right = (jax.nn.sigmoid(right_raw[:hidden]) * right_raw[hidden:] * keep[None]).astype(
        jnp.bfloat16
    )
    gate = jax.nn.sigmoid(
        jnp.dot(normed, proj[:, 4 * hidden :], preferred_element_type=jnp.float32)
    )
    return (left, right, gate)


def finish(pair, product, gate, mid_gain, final):
    group = product.shape[0]
    total = group * lax.axis_size("chan")
    first, second = (
        lax.psum(jnp.sum(product, axis=0).astype(jnp.bfloat16), "chan").astype(jnp.float32),
        lax.psum(jnp.sum(product * product, axis=0).astype(jnp.bfloat16), "chan").astype(
            jnp.float32
        ),
    )
    mean = first / total
    var = second / total - mean * mean
    offset = lax.axis_index("chan") * group
    gain_part = lax.dynamic_slice_in_dim(mid_gain, offset, group, 0)
    final_part = lax.dynamic_slice_in_dim(final, offset, group, 0)
    normed = ((product - mean) / jnp.sqrt(var + 1e-05) * gain_part[:, None, None]).astype(
        jnp.bfloat16
    )
    summed = lax.psum_scatter(
        jnp.einsum("crj,cd->jrd", normed, final_part, preferred_element_type=jnp.float32).astype(
            jnp.bfloat16
        ),
        "chan",
        scatter_dimension=0,
        tiled=True,
    ).astype(jnp.float32)
    update = jnp.transpose(summed, (1, 0, 2))
    return (pair.astype(jnp.float32) + gate * update).astype(jnp.bfloat16)


def shards(
    pair,
    pair_mask,
    out_in_gain,
    out_proj,
    out_mid_gain,
    out_final,
    in_in_gain,
    in_proj,
    in_mid_gain,
    in_final,
):
    left, right, gate = project(
        pair, pair_mask, out_in_gain, out_proj, "rqd,de->erq", "rqd,de->erq", False
    )
    left, right = (
        lax.all_to_all(left, "chan", split_axis=0, concat_axis=2, tiled=True),
        lax.all_to_all(right, "chan", split_axis=0, concat_axis=2, tiled=True),
    )
    product = jnp.einsum(
        "cik,cjk->cij",
        left,
        lax.all_gather(right, ("row", "sub"), axis=1, tiled=True),
        preferred_element_type=jnp.float32,
    )
    middle = finish(pair, product, gate, out_mid_gain, out_final)
    left_in, right_in, gate_in = project(
        middle, pair_mask, in_in_gain, in_proj, "rqd,de->eqr", "rqd,de->erq", True
    )
    columns = lax.all_to_all(
        lax.all_to_all(left_in, "chan", split_axis=0, concat_axis=1, tiled=True),
        ("row", "sub"),
        split_axis=1,
        concat_axis=2,
        tiled=True,
    )
    right_in = lax.all_to_all(right_in, "chan", split_axis=0, concat_axis=2, tiled=True)
    product_in = jnp.einsum(
        "cik,ckj->cij",
        columns,
        lax.all_gather(right_in, ("row", "sub"), axis=1, tiled=True),
        preferred_element_type=jnp.float32,
    )
    return finish(middle, product_in, gate_in, in_mid_gain, in_final)


def solution(mesh):
    placed = (
        P(("parts", "row", "sub"), "chan", None),
        P(("parts", "row", "sub"), "chan"),
        P(),
        P(),
        P(),
        P(),
        P(),
        P(),
        P(),
        P(),
    )
    return jax.shard_map(
        shards,
        mesh=mesh,
        in_specs=placed,
        out_specs=P(("parts", "row", "sub"), "chan", None),
        check_vma=False,
    )
```

profile of v0, /device:TPU:0, one launch (start us, length us, event | category | flops | bytes accessed | tf_op | source)
XLA Modules:
  0.0 842.3 jit_solution(12634183757078182451)
XLA Ops:
  6.5 0.0 copy-start
  6.5 0.0 all-gather.3.cloned.1.call-start
  6.6 2.1 convert_reduce_fusion.1
  8.7 3.1 fusion.7
  11.9 0.0 copy-done.2
  11.9 0.0 copy-done.12
  11.9 0.0 copy-done.10
  11.9 1.9 convolution_bitcast_fusion.3
  13.8 0.0 copy-start.7
  13.8 1.9 convolution_bitcast_fusion.2
  15.6 0.0 copy-done.7
  15.7 2.9 fusion.23
  18.6 0.0 all-gather.3.cloned.1.call-update
  18.6 0.2 all-gather.5.cloned.1.call-start
  18.9 3.2 copy.24
  22.1 279.2 %all-gather.3.cloned.1.call-done = bf16[128,448,448]{0,2,1:T(8,128)(2,1)} async-done(((bf16[128,14,448]{0,2,1:T(8,128)(2,1)}), bf16[128,448,448]{0,2,1:T(8,128)(2,1)}) %all-gather.3.cloned.1.call-update) | async-done | bytes 51380240 | tf_op jit(solution)/shard_map/all_gather | solution.py:85
  301.4 79.1 %copy.25 = bf16[128,448,448]{2,1,0:T(8,128)(2,1)} copy(bf16[128,448,448]{0,2,1:T(8,128)(2,1)} %all-gather.3.cloned.1.call-done) | data formatting | bytes 102760448 | tf_op jit(solution)/shard_map/all_gather | solution.py:85
  380.5 23.2 %fusion.63 = (bf16[14,448]{1,0:T(8,128)(2,1)S(1)}, bf16[14,448]{1,0:T(8,128)(2,1)S(1)}, f32[128,14,448]{2,1,0:T(8,128)S(1)}) fusion(bf16[128,14,448]{2,1,0:T(8,128)(2,1)} %copy.24, bf16[128,448,448]{2,1,0:T(8,128)(2,1)} %copy.25), kind=kOutput, calls=%fused_computation.84 | convolution fusion | flops 721719040 | bytes 56222208 | tf_op jit(solution)/shard_map/cik,cjk->cij/dot_general | solution.py:82
  403.7 0.0 copy-done.8
  403.7 0.5 multiply_convert_fusion.1
  404.2 0.0 copy-start.3
  404.2 2.2 fusion.36
  406.4 0.0 copy-start.11
  406.5 0.0 copy-start.13
  406.5 2.9 convert_reduce_fusion
  409.3 0.0 copy-start.4
  409.4 2.0 fusion.4
  411.4 1.9 convolution_bitcast_fusion
  413.3 1.9 fusion.13
  415.2 0.0 all-gather.5.cloned.1.call-update
  415.2 1.9 convolution_bitcast_fusion.1
  417.1 1.4 fusion.18
  418.5 1.1 copy.27
  419.6 80.0 %all_to_all.18 = bf16[128,448,14]{0,2,1:T(8,128)(2,1)S(1)} all-to-all(bf16[128,448,14]{0,2,1:T(8,128)(2,1)S(1)} %copy.27), channel_id=1, replica_groups=mesh['parts'=1,'row'=16,'chan'=1,'sub'=2] {'row','sub'}, dimensions={1} | all-to-all | bytes 3211264 | tf_op jit(solution)/shard_map/all_to_all | solution.py:92
  499.6 0.5 copy.29
  500.0 1.4 all_to_all.16
  501.4 3.7 copy.30
  505.1 224.0 %all-gather.5.cloned.1.call-done = bf16[128,448,448]{0,2,1:T(8,128)(2,1)} async-done(((bf16[128,14,448]{0,2,1:T(8,128)(2,1)}), bf16[128,448,448]{0,2,1:T(8,128)(2,1)}) %all-gather.5.cloned.1.call-update) | async-done | bytes 51380240 | tf_op jit(solution)/shard_map/all_gather | solution.py:103
  729.1 79.1 %copy.31 = bf16[128,448,448]{2,1,0:T(8,128)(2,1)} copy(bf16[128,448,448]{0,2,1:T(8,128)(2,1)} %all-gather.5.cloned.1.call-done) | data formatting | bytes 102760448 | tf_op jit(solution)/shard_map/all_gather | solution.py:103
  808.2 20.7 %fusion.62 = (bf16[14,448]{1,0:T(8,128)(2,1)S(1)}, bf16[14,448]{1,0:T(8,128)(2,1)S(1)}, f32[128,14,448]{2,1,0:T(8,128)S(1)}) fusion(bf16[128,14,448]{2,1,0:T(8,128)(2,1)S(1)} %copy.30, bf16[128,448,448]{2,1,0:T(8,128)(2,1)} %copy.31), kind=kOutput, calls=%fused_computation.83 | convolution fusion | flops 721719040 | bytes 56222208 | tf_op jit(solution)/shard_map/cik,ckj->cij/dot_general | solution.py:100
  829.0 0.0 copy-start.6
  829.0 0.5 multiply_convert_fusion
  829.5 0.2 copy-done.6
  829.7 2.2 fusion.39
  831.9 0.0 copy-done.5
  831.9 0.0 copy-start.1
  831.9 3.5 fusion.11
  835.4 0.0 copy-done.1
  (19 shorter events, 0.1 us)
Async XLA Ops:
  6.5 397.7 %copy-start = (bf16[128,128]{1,0:T(8,128)(2,1)S(1)}, bf16[128,128]{1,0:T(8,128)(2,1)}, u32[]{:S(2)}) copy-start(bf16[128,128]{1,0:T(8,128)(2,1)} %param.15) | copy-start | bytes 98308
  6.5 5.3 copy-start.2
  6.5 5.3 copy-start.12
  6.5 5.4 copy-start.10
  6.5 294.8 %all-gather.3.cloned.1.call-start = ((), (), s32[]{:S(2)}) async-start(), calls=%async_computation.1 | async-start | bytes 52985856 | tf_op jit(solution)/shard_map/all_gather | solution.py:85
  13.8 1.9 copy-start.7
  18.6 710.5 %all-gather.5.cloned.1.call-start = ((), (), s32[]{:S(2)}) async-start(), calls=%async_computation.2 | async-start | bytes 52985856 | tf_op jit(solution)/shard_map/all_gather | solution.py:103
  380.5 23.2 %copy-start.8 = (f32[128]{0:T(128)S(1)}, f32[128]{0:T(128)}, u32[]{:S(2)}) copy-start(f32[128]{0:T(128)} %param.14) | copy-start | bytes 1540
  404.2 2.2 copy-start.3
  406.4 5.0 copy-start.11
  406.5 5.0 copy-start.13
  409.3 5.9 copy-start.4
  808.2 20.8 %copy-start.9 = (f32[128]{0:T(128)S(1)}, f32[128]{0:T(128)}, u32[]{:S(2)}) copy-start(f32[128]{0:T(128)} %param.18) | copy-start | bytes 1540
  829.0 0.8 copy-start.6
  829.7 2.2 copy-start.5
  831.9 3.5 copy-start.1
Sparse Core Ops, SparseCore 0:
  18.8 282.5 all-gather.2
  415.4 313.7 all-gather.4
where the time goes:
time: 846 us; the launch traced here: 842 us
  waiting for transfers between devices  503 us (59%)
  local copies, waits for them, and re-layouts  168 us (20%)
  blocking collectives  80 us (9%)
  matrix products  62.1 us (7%)
  other arithmetic  14.6 us (2%)
  between operations  13.7 us (2%)
    all_gather x1, waiting for transfers between devices, shards(): lax.all_gather(right, ('row', 'sub'), axis=1, tiled=True)  279 us
    all_gather x1, waiting for transfers between devices, shards(): lax.all_gather(right_in, ('row', 'sub'), axis=1, tiled=True)  224 us
    all_to_all x1, blocking collectives, shards(): lax.all_to_all(lax.all_to_all(left_in, 'chan', split_axis=0, concat_axis=...  80 us
    all_gather x1, local copies, waits for them, and re-layouts, shards(): lax.all_gather(right, ('row', 'sub'), axis=1, tiled=True)  79.1 us
    all_gather x1, local copies, waits for them, and re-layouts, shards(): lax.all_gather(right_in, ('row', 'sub'), axis=1, tiled=True)  79.1 us
    dot_general x1, matrix products, shards(): jnp.einsum('cik,cjk->cij', left, lax.all_gather(right, ('row', 'sub'), ax...  23.2 us
    dot_general x1, matrix products, shards(): jnp.einsum('cik,ckj->cij', columns, lax.all_gather(right_in, ('row', 'sub...  20.7 us
  transfers between devices with their start and end apart: 2, of which 2 were waited for; matrix products, arithmetic and copies ran while one was open for 1% of the time, Pallas kernels for 0%

commit v1 on v0

--- a/solution.py
+++ b/solution.py
@@ -2,6 +2,16 @@
 import jax.numpy as jnp
 from jax import lax
 from jax.sharding import PartitionSpec as P
+
+push_shapes_up = lambda here_x: jnp.concatenate(
+    jax.lax.all_to_all(
+        jnp.stack(jax.lax.psum(1, axis_name=("row", "sub")) * [here_x]),
+        axis_name=("row", "sub"),
+        split_axis=0,
+        concat_axis=0,
+    ),
+    axis=1,
+)
 
 
 def norm_last(values, gain):
@@ -98,10 +108,7 @@
     )
     right_in = lax.all_to_all(right_in, "chan", split_axis=0, concat_axis=2, tiled=True)
     product_in = jnp.einsum(
-        "cik,ckj->cij",
-        columns,
-        lax.all_gather(right_in, ("row", "sub"), axis=1, tiled=True),
-        preferred_element_type=jnp.float32,
+        "cik,ckj->cij", columns, push_shapes_up(right_in), preferred_element_type=jnp.float32
     )
     return finish(middle, product_in, gate_in, in_mid_gain, in_final)
 

time: 846 us -> 1750 us (2.07)
  waiting for transfers between devices: 503 us -> 1460 us
  blocking collectives: 80 us -> 0 us
  local copies, waits for them, and re-layouts: 168 us -> 189 us
    all_to_all x0 -> x2, waiting for transfers between devices: none -> 1180 us  [the longest x1 1140 us: jax.lax.all_to_all(jnp.stack(jax.lax.psum(1, axis_name=('row', 'sub')) *...]
    all_gather x1 -> x0, waiting for transfers between devices: 224 us -> none  [shards(): lax.all_gather(right_in, ('row', 'sub'), axis=1, tiled=True)]
    all_to_all x1 -> x0, blocking collectives: 80 us -> none  [shards(): lax.all_to_all(lax.all_to_all(left_in, 'chan', split_axis=0, concat_axis=...]
    all_gather x1 -> x0, local copies, waits for them, and re-layouts: 79.1 us -> none  [shards(): lax.all_gather(right_in, ('row', 'sub'), axis=1, tiled=True)]
    reshape x0 -> x1, local copies, waits for them, and re-layouts: none -> 78.8 us  [jnp.concatenate(jax.lax.all_to_all(jnp.stack(jax.lax.psum(1, axis_name=('...]
  transfers between devices with their start and end apart: 2 -> 3, of which waited for: 2 -> 3; matrix products, arithmetic and copies ran while one was open for 1% -> 1% of each run, Pallas kernels for 0% -> 0%
where the time goes in v1:
time: 1750 us
  waiting for transfers between devices  1460 us (83%)
  local copies, waits for them, and re-layouts  189 us (11%)
  matrix products  65.3 us (4%)
    all_to_all x1, waiting for transfers between devices, jax.lax.all_to_all(jnp.stack(jax.lax.psum(1, axis_name=('row', 'sub')) *...  1140 us
    all_gather x1, waiting for transfers between devices, shards(): lax.all_gather(right, ('row', 'sub'), axis=1, tiled=True)  279 us
    reshape x1, local copies, waits for them, and re-layouts, jnp.concatenate(jax.lax.all_to_all(jnp.stack(jax.lax.psum(1, axis_name=('...  78.8 us
    all_gather x1, local copies, waits for them, and re-layouts, shards(): lax.all_gather(right, ('row', 'sub'), axis=1, tiled=True)  78.8 us
    all_to_all x1, waiting for transfers between devices, shards(): lax.all_to_all(lax.all_to_all(left_in, 'chan', split_axis=0, concat_axis=...  39.2 us
  transfers between devices with their start and end apart: 3, of which 3 were waited for; matrix products, arithmetic and copies ran while one was open for 1% of the time, Pallas kernels for 0%

profile of v1, /device:TPU:0, one launch (start us, length us, event | category | flops | bytes accessed | tf_op | source)
XLA Modules:
  0.0 1749.8 jit_solution(7985218156106140852)
XLA Ops:
  6.5 0.0 all-gather.2.cloned.1.call-start
  6.6 2.1 convert_reduce_fusion.1
  8.7 0.0 copy-start.8
  8.7 3.1 fusion.7
  11.9 0.0 copy-done.2
  11.9 0.0 copy-done.19
  11.9 0.0 copy-done.18
  11.9 0.0 copy-start.14
  11.9 1.9 convolution_bitcast_fusion.3
  13.8 0.0 copy-done.8
  13.8 0.0 copy-done.14
  13.8 0.0 copy-start.11
  13.8 1.9 convolution_bitcast_fusion.2
  15.7 2.9 fusion.23
  18.7 0.0 all-gather.2.cloned.1.call-update
  18.7 3.2 copy.24
  21.9 279.5 %all-gather.2.cloned.1.call-done = bf16[128,448,448]{0,2,1:T(8,128)(2,1)} async-done(((bf16[128,14,448]{0,2,1:T(8,128)(2,1)}), bf16[128,448,448]{0,2,1:T(8,128)(2,1)}) %all-gather.2.cloned.1.call-update) | async-done | bytes 51380240 | tf_op jit(solution)/shard_map/all_gather | solution.py:95
  301.4 78.8 %copy.25 = bf16[128,448,448]{2,1,0:T(8,128)(2,1)} copy(bf16[128,448,448]{0,2,1:T(8,128)(2,1)} %all-gather.2.cloned.1.call-done) | data formatting | bytes 102760448 | tf_op jit(solution)/shard_map/all_gather | solution.py:95
  380.2 23.2 %fusion.63 = (bf16[14,448]{1,0:T(8,128)(2,1)S(1)}, bf16[14,448]{1,0:T(8,128)(2,1)S(1)}, f32[128,14,448]{2,1,0:T(8,128)S(1)}) fusion(bf16[128,14,448]{2,1,0:T(8,128)(2,1)} %copy.24, bf16[128,448,448]{2,1,0:T(8,128)(2,1)} %copy.25), kind=kOutput, calls=%fused_computation.84 | convolution fusion | flops 721719040 | bytes 56222208 | tf_op jit(solution)/shard_map/cik,cjk->cij/dot_general | solution.py:92
  403.4 0.5 multiply_convert_fusion.1
  403.9 0.0 copy-start.3
  404.0 2.2 fusion.36
  406.2 0.0 copy-start.20
  406.2 3.6 convert_reduce_fusion
  409.9 0.0 copy-start.4
  409.9 0.0 copy-start.6
  409.9 2.2 fusion.4
  412.1 2.7 convolution_bitcast_fusion.1
  414.9 1.1 fusion.18
  416.0 2.3 copy.27
  418.3 2.8 all-to-all-start
  421.1 2.7 convolution_bitcast_fusion
  423.8 1.1 fusion.13
  425.0 39.2 %all-to-all-done = bf16[128,448,14]{0,2,1:T(8,128)(2,1)S(1)} async-done(((bf16[128,448,14]{0,2,1:T(8,128)(2,1)}), bf16[128,448,14]{0,2,1:T(8,128)(2,1)S(1)}, u32[]{:S(2)}, u32[]{:S(2)}) %all-to-all-start) | async-done | bytes 1605664 | tf_op jit(solution)/shard_map/all_to_all | solution.py:102
  464.2 16.4 stack.2
  480.6 4.9 all-to-all-start.1
  485.5 1.7 copy.29
  487.2 3.6 all_to_all.19
  490.9 3.5 copy.30
  494.4 1141.8 %all-to-all-done.1 = bf16[32,128,14,448]{1,3,2,0:T(8,128)(2,1)} async-done(((bf16[32,128,14,448]{1,3,2,0:T(8,128)(2,1)}), bf16[32,128,14,448]{1,3,2,0:T(8,128)(2,1)}, u32[]{:S(2)}, u32[]{:S(2)}) %all-to-all-start.1) | async-done | bytes 51380256 | tf_op jit(solution)/shard_map/all_to_all | solution.py:7
  1636.2 78.8 %copy.31 = bf16[128,448,448]{2,1,0:T(8,128)(2,1)} copy(bf16[128,448,448]{0,2,1:T(8,128)(2,1)} %bitcast.16) | data formatting | bytes 102760448 | tf_op jit(solution)/shard_map/reshape | solution.py:6
  1715.0 20.7 %fusion.62 = (bf16[14,448]{1,0:T(8,128)(2,1)S(1)}, bf16[14,448]{1,0:T(8,128)(2,1)S(1)}, f32[128,14,448]{2,1,0:T(8,128)S(1)}) fusion(bf16[128,14,448]{2,1,0:T(8,128)(2,1)S(1)} %copy.30, bf16[128,448,448]{2,1,0:T(8,128)(2,1)} %copy.31), kind=kOutput, calls=%fused_computation.83 | convolution fusion | flops 721719040 | bytes 56222208 | tf_op jit(solution)/shard_map/cik,ckj->cij/dot_general | solution.py:110
  1735.7 0.0 copy-start.10
  1735.8 0.5 multiply_convert_fusion
  1736.3 0.2 copy-done.10
  1736.5 2.2 fusion.39
  1738.7 0.0 copy-start.1
  1738.7 4.3 fusion.11
  (34 shorter events, 0.1 us)
Async XLA Ops:
  6.5 397.4 %copy-start = (bf16[128,128]{1,0:T(8,128)(2,1)S(1)}, bf16[128,128]{1,0:T(8,128)(2,1)}, u32[]{:S(2)}) copy-start(bf16[128,128]{1,0:T(8,128)(2,1)} %param.15) | copy-start | bytes 98308
  6.5 5.3 copy-start.2
  6.5 5.4 copy-start.19
  6.5 5.4 copy-start.18
  6.5 294.8 %all-gather.2.cloned.1.call-start = ((), (), s32[]{:S(2)}) async-start(), calls=%async_computation.2 | async-start | bytes 52985856 | tf_op jit(solution)/shard_map/all_gather | solution.py:95
  8.7 5.1 copy-start.8
  11.9 1.9 copy-start.14
  13.8 1.9 copy-start.11
  380.2 23.2 %copy-start.16 = (f32[128]{0:T(128)S(1)}, f32[128]{0:T(128)}, u32[]{:S(2)}) copy-start(f32[128]{0:T(128)} %param.14) | copy-start | bytes 1540
  403.9 2.2 copy-start.3
  404.0 2.2 copy-start.9
  404.0 2.2 copy-start.15
  406.2 5.9 copy-start.20
  409.9 11.3 copy-start.4
  409.9 11.2 copy-start.6
  412.1 2.7 copy-start.12
  416.0 5.1 copy-start.13
  418.3 45.9 %all-to-all-start = ((bf16[128,448,14]{0,2,1:T(8,128)(2,1)}), bf16[128,448,14]{0,2,1:T(8,128)(2,1)S(1)}, u32[]{:S(2)}, u32[]{:S(2)}) async-start(bf16[128,448,14]{0,2,1:T(8,128)(2,1)} %copy.27), calls=%async_computation | async-start | bytes 3670016 | tf_op jit(solution)/shard_map/all_to_all | solution.py:102
  480.6 1155.6 %all-to-all-start.1 = ((bf16[32,128,14,448]{1,3,2,0:T(8,128)(2,1)}), bf16[32,128,14,448]{1,3,2,0:T(8,128)(2,1)}, u32[]{:S(2)}, u32[]{:S(2)}) async-start(bf16[32,128,14,448]{1,3,2,0:T(8,128)(2,1)} %stack.2), calls=%async_computation.1 | async-start | bytes 102760448 | tf_op jit(solution)/shard_map/all_to_all | solution.py:7
  1715.0 20.8 %copy-start.17 = (f32[128]{0:T(128)S(1)}, f32[128]{0:T(128)}, u32[]{:S(2)}) copy-start(f32[128]{0:T(128)} %param.18) | copy-start | bytes 1540
  1735.7 0.8 copy-start.10
  1736.5 2.2 copy-start.5
  1736.5 2.2 copy-start.7
  1738.7 4.3 copy-start.1
Sparse Core Ops, SparseCore 0:
  18.8 282.5 all-gather.1
